TPU v7x, 32 devices: a whole 2x2x4 slice. The times are simulated.
32 devices in a mesh: dp: 16 (over z, y, core), seq: 2 (over x).
Axes of the slice: x: 2, y: 2, z: 4, core: 2. Of those that a mesh axis runs over, the one named last changes fastest.
Arguments:
- inputs: bfloat16 [2, 2048, 1024], P(None, ('dp', 'seq')), may hold values from -6 to 6
- cotangent: bfloat16 [2, 2048, 1024], P(None, ('dp', 'seq')), may hold values from -6 to 6
- w_qkv: bfloat16 [1024, 3072], P('dp'), may hold values from -0.1875 to 0.1875
- w_out: bfloat16 [1024, 1024], P('dp'), may hold values from -0.75 to 0.75
- w_up: bfloat16 [1024, 4096], P('dp'), may hold values from -0.1875 to 0.1875
- w_down: bfloat16 [4096, 1024], P('dp'), may hold values from -0.09375 to 0.09375
- bias_q: bfloat16 [1024], P('dp'), may hold values from -3 to 3
- bias_v: bfloat16 [1024], P('dp'), may hold values from -3 to 3
- bias_out: bfloat16 [1024], P('dp'), may hold values from -3 to 3
- gain_one: bfloat16 [1024], P('dp'), may hold values from 0.5 to 1.5
- shift_one: bfloat16 [1024], P('dp'), may hold values from -3 to 3
- bias_up: bfloat16 [4096], P('dp'), may hold values from -3 to 3
- bias_down: bfloat16 [1024], P('dp'), may hold values from -3 to 3
- gain_two: bfloat16 [1024], P('dp'), may hold values from 0.5 to 1.5
- shift_two: bfloat16 [1024], P('dp'), may hold values from -3 to 3
Outputs:
- layer_out: bfloat16 [2, 2048, 1024], P(None, ('dp', 'seq'))
- input_grad: float32 [2, 2048, 1024], P(None, ('dp', 'seq'))
- grad_qkv: float32 [1024, 3072], P('dp')
- grad_out: float32 [1024, 1024], P('dp')
- grad_up: float32 [1024, 4096], P('dp')
- grad_down: float32 [4096, 1024], P('dp')
- grad_bias_q: float32 [1024], P('dp')
- grad_bias_v: float32 [1024], P('dp')
- grad_bias_out: float32 [1024], P('dp')
- grad_gain_one: float32 [1024], P('dp')
- grad_shift_one: float32 [1024], P('dp')
- grad_bias_up: float32 [4096], P('dp')
- grad_bias_down: float32 [1024], P('dp')
- grad_gain_two: float32 [1024], P('dp')
- grad_shift_two: float32 [1024], P('dp')
All inputs are finite; a program needn't handle non-finite values.
Results may differ from a plain program's by a relative error of at most 0.015.
Values may be sent and summed in bfloat16 or wider, within the bound.
No kernel may reach another device: no remote copies, remote signals or barrier semaphores. Data moves between devices by JAX's collectives and lax.ppermute only.
A program may use at most 192 MiB of HBM per device.

v0:
```python
import math
import jax
import jax.numpy as jnp
from jax import lax
from jax.sharding import PartitionSpec as P

HEAD = 64


def for_sending(shard):

    def short(part):
        return part.astype(jnp.bfloat16) if part.dtype == jnp.float32 else part

    return jax.tree.map(short, shard)


def normalize(features, gain, shift):
    centre = jnp.mean(features, axis=-1, keepdims=True)
    centred = features - centre
    spread = jnp.mean(centred * centred, axis=-1, keepdims=True)
    return centred * lax.rsqrt(spread + 1e-12) * gain + shift


def gelu_exact(values):
    return 0.5 * values * (1.0 + jax.scipy.special.erf(values * (1.0 / math.sqrt(2.0))))


def times_back(left, right):
    return lax.dot_general(
        left, right, (((1,), (1,)), ((), ())), preferred_element_type=jnp.float32
    )


def inner_rows(left, right):
    return lax.dot_general(
        left, right, (((0,), (0,)), ((), ())), preferred_element_type=jnp.float32
    )


def add_up(first_term, second_term):
    return first_term + second_term


def per_device(
    inputs,
    cotangent,
    w_qkv,
    w_out,
    w_up,
    w_down,
    bias_q,
    bias_v,
    bias_out,
    gain_one,
    shift_one,
    bias_up,
    bias_down,
    gain_two,
    shift_two,
):
    shards = (
        w_qkv,
        w_out,
        w_up,
        w_down,
        bias_q,
        bias_v,
        bias_out,
        gain_one,
        shift_one,
        bias_up,
        bias_down,
        gain_two,
        shift_two,
    )
    width = w_qkv.shape[1] // 3
    heads = width // HEAD
    scale = 1.0 / math.sqrt(HEAD)
    micro = inputs.shape[0]
    kept = []
    vector_total = None
    outputs = []
    input_grads = []
    for index in range(micro):
        full = (
            lax.all_gather(shards[0], "dp", axis=0, tiled=True),
            lax.all_gather(shards[1], "dp", axis=0, tiled=True),
            lax.all_gather(shards[2], "dp", axis=0, tiled=True),
            lax.all_gather(shards[3], "dp", axis=0, tiled=True),
            lax.all_gather(shards[4], "dp", axis=0, tiled=True),
            lax.all_gather(shards[5], "dp", axis=0, tiled=True),
            lax.all_gather(shards[6], "dp", axis=0, tiled=True),
            lax.all_gather(shards[7], "dp", axis=0, tiled=True),
            lax.all_gather(shards[8], "dp", axis=0, tiled=True),
            lax.all_gather(shards[9], "dp", axis=0, tiled=True),
            lax.all_gather(shards[10], "dp", axis=0, tiled=True),
            lax.all_gather(shards[11], "dp", axis=0, tiled=True),
            lax.all_gather(shards[12], "dp", axis=0, tiled=True),
        )
        full_qkv, full_out, full_up, full_down = (full[0], full[1], full[2], full[3])
        (
            query_bias,
            value_bias,
            out_bias,
            first_gain,
            first_shift,
            up_bias,
            down_bias,
            second_gain,
            second_shift,
        ) = [item.astype(jnp.float32) for item in full[4:]]
        tokens = inputs[index]
        rows = tokens.shape[0]
        qkv = jnp.dot(tokens, full_qkv, preferred_element_type=jnp.float32)
        queries = (qkv[:, :width] + query_bias).astype(jnp.bfloat16)
        keys = qkv[:, width : 2 * width].astype(jnp.bfloat16)
        values = (qkv[:, 2 * width :] + value_bias).astype(jnp.bfloat16)
        all_keys, all_values = (
            lax.all_gather(keys, "seq", axis=0, tiled=True),
            lax.all_gather(values, "seq", axis=0, tiled=True),
        )
        length = all_keys.shape[0]
        query_heads = queries.reshape(rows, heads, HEAD)
        key_heads = all_keys.reshape(length, heads, HEAD)
        value_heads = all_values.reshape(length, heads, HEAD)
        scores = (
            jnp.einsum("qhd,khd->hqk", query_heads, key_heads, preferred_element_type=jnp.float32)
            * scale
        )
        top = jnp.max(scores, axis=-1, keepdims=True)
        log_norm = top + jnp.log(jnp.sum(jnp.exp(scores - top), axis=-1, keepdims=True))
        probs = jnp.exp(scores - log_norm)
        probs_low = probs.astype(jnp.bfloat16)
        context = (
            jnp.einsum("hqk,khd->qhd", probs_low, value_heads, preferred_element_type=jnp.float32)
            .reshape(rows, width)
            .astype(jnp.bfloat16)
        )
        attended = jnp.dot(context, full_out, preferred_element_type=jnp.float32) + out_bias
        resid_one = tokens.astype(jnp.float32) + attended
        first = normalize(resid_one, first_gain, first_shift)
        first_low = first.astype(jnp.bfloat16)
        pre_act = jnp.dot(first_low, full_up, preferred_element_type=jnp.float32) + up_bias
        act = gelu_exact(pre_act).astype(jnp.bfloat16)
        mlp = jnp.dot(act, full_down, preferred_element_type=jnp.float32) + down_bias
        resid_two = first + mlp
        second = normalize(resid_two, second_gain, second_shift)
        outputs.append(second.astype(jnp.bfloat16))
        again = (
            lax.all_gather(w_qkv, "dp", axis=0, tiled=True),
            lax.all_gather(w_out, "dp", axis=0, tiled=True),
            lax.all_gather(w_up, "dp", axis=0, tiled=True),
            lax.all_gather(w_down, "dp", axis=0, tiled=True),
        )
        full_qkv, full_out, full_up, full_down = (again[0], again[1], again[2], again[3])
        incoming = cotangent[index].astype(jnp.float32)
        _, pull_two = jax.vjp(normalize, resid_two, second_gain, second_shift)
        grad_resid_two, grad_gain_b, grad_shift_b = pull_two(incoming)
        grad_mlp = grad_resid_two.astype(jnp.bfloat16)
        grad_act = times_back(grad_mlp, full_down)
        _, pull_gelu = jax.vjp(gelu_exact, pre_act)
        grad_pre = pull_gelu(grad_act)[0].astype(jnp.bfloat16)
        grad_first = grad_resid_two + times_back(grad_pre, full_up)
        _, pull_one = jax.vjp(normalize, resid_one, first_gain, first_shift)
        grad_resid_one, grad_gain_a, grad_shift_a = pull_one(grad_first)
        grad_attended = grad_resid_one.astype(jnp.bfloat16)
        grad_context = times_back(grad_attended, full_out).astype(jnp.bfloat16)
        grad_ctx_heads = grad_context.reshape(rows, heads, HEAD)
        grad_probs = jnp.einsum(
            "qhd,khd->hqk", grad_ctx_heads, value_heads, preferred_element_type=jnp.float32
        )
        grad_scores = (
            probs * (grad_probs - jnp.sum(probs * grad_probs, axis=-1, keepdims=True))
        ).astype(jnp.bfloat16)
        grad_queries = (
            (
                jnp.einsum(
                    "hqk,khd->qhd", grad_scores, key_heads, preferred_element_type=jnp.float32
                )
                * scale
            )
            .reshape(rows, width)
            .astype(jnp.bfloat16)
        )
        key_part = (
            jnp.einsum(
                "hqk,qhd->khd", grad_scores, query_heads, preferred_element_type=jnp.float32
            ).reshape(length, width)
            * scale
        )
        value_part = jnp.einsum(
            "hqk,qhd->khd", probs_low, grad_ctx_heads, preferred_element_type=jnp.float32
        ).reshape(length, width)
        grad_keys, grad_values = (
            lax.psum_scatter(
                key_part.astype(jnp.bfloat16), "seq", scatter_dimension=0, tiled=True
            ).astype(jnp.float32),
            lax.psum_scatter(
                value_part.astype(jnp.bfloat16), "seq", scatter_dimension=0, tiled=True
            ).astype(jnp.float32),
        )
        grad_values = grad_values.astype(jnp.bfloat16)
        grad_tokens = jnp.concatenate(
            [grad_queries, grad_keys.astype(jnp.bfloat16), grad_values], axis=1
        )
        input_grads.append(grad_resid_one + times_back(grad_tokens, full_qkv))
        vector_part = (
            jnp.sum(grad_queries.astype(jnp.float32), axis=0),
            jnp.sum(grad_values.astype(jnp.float32), axis=0),
            jnp.sum(grad_attended.astype(jnp.float32), axis=0),
            grad_gain_a,
            grad_shift_a,
            jnp.sum(grad_pre.astype(jnp.float32), axis=0),
            jnp.sum(grad_mlp.astype(jnp.float32), axis=0),
            grad_gain_b,
            grad_shift_b,
        )
        if vector_total is None:
            vector_total = vector_part
        else:
            vector_total = jax.tree.map(add_up, vector_total, vector_part)
        kept.append(
            (tokens, grad_tokens, context, grad_attended, first_low, grad_pre, act, grad_mlp)
        )
    stacked = [jnp.concatenate([entry[slot] for entry in kept], axis=0) for slot in range(8)]
    totals = (
        inner_rows(stacked[0], stacked[1]),
        inner_rows(stacked[2], stacked[3]),
        inner_rows(stacked[4], stacked[5]),
        inner_rows(stacked[6], stacked[7]),
    ) + tuple(vector_total)
    shares = lax.psum_scatter(totals, "dp", scatter_dimension=0, tiled=True)
    final = jax.tree.map(
        lambda part: part.astype(jnp.float32), lax.psum(for_sending(shares), "seq")
    )
    return (
        jnp.stack(outputs),
        jnp.stack(input_grads),
        final[0],
        final[1],
        final[2],
        final[3],
        final[4],
        final[5],
        final[6],
        final[7],
        final[8],
        final[9],
        final[10],
        final[11],
        final[12],
    )


def solution(mesh):
    placed = (
        P(None, ("dp", "seq"), None),
        P(None, ("dp", "seq"), None),
        P("dp", None),
        P("dp", None),
        P("dp", None),
        P("dp", None),
        P("dp"),
        P("dp"),
        P("dp"),
        P("dp"),
        P("dp"),
        P("dp"),
        P("dp"),
        P("dp"),
        P("dp"),
    )
    return jax.shard_map(
        per_device,
        mesh=mesh,
        in_specs=placed,
        out_specs=(
            P(None, ("dp", "seq"), None),
            P(None, ("dp", "seq"), None),
            P("dp", None),
            P("dp", None),
            P("dp", None),
            P("dp", None),
            P("dp"),
            P("dp"),
            P("dp"),
            P("dp"),
            P("dp"),
            P("dp"),
            P("dp"),
            P("dp"),
            P("dp"),
        ),
        check_vma=False,
    )
```

profile of v0, /device:TPU:0, one launch (start us, length us, event | category | flops | bytes accessed | tf_op | source)
XLA Modules:
  0.0 1044.0 jit_solution(4009803265087155789)
XLA Ops:
  18.7 64.1 %all-reduce.18 = (bf16[1024]{0:T(1024)(128)(2,1)S(1)}, bf16[1024]{0:T(1024)(128)(2,1)S(1)}, bf16[1024]{0:T(1024)(128)(2,1)S(1)}, bf16[1024]{0:T(1024)(128)(2,1)S...) all-reduce(bf16[1024]{0:T(1024)(128)(2,1)S(1)} %dynamic-update-slic, ...), channel_id=1, replica_groups=mesh['dp'=16,'seq'=2] {'dp'}, use_global_device_ids=true, to_apply=%add | all-reduce | flops 8192 | bytes 32768
  84.6 17.2 %all-gather = bf16[16,1,256]{2,1,0:T(2,128)(2,1)S(1)} all-gather(bf16[1,1,256]{2,1,0:T(2,128)(2,1)S(1)} %reshape.260), channel_id=1, replica_groups=mesh['dp'=16,'seq'=2] {'dp'}, dimensions={0}, use_global_device_ids=true | all-gather | bytes 8704 | tf_op jit(solution)/shard_map/all_gather | solution.py:96
  110.4 6.4 all_gather.88
  117.0 5.7 all_gather.87
  123.1 5.6 all_gather.76
  128.9 6.2 all_gather.36
  143.7 50.2 %all-gather.10.cloned.1.call-done = bf16[1024,4096]{1,0:T(8,128)(2,1)} async-done(((bf16[64,4096]{1,0:T(8,128)(2,1)}), bf16[1024,4096]{1,0:T(8,128)(2,1)}) %all-gather.10.cloned.1.call-update) | async-done | bytes 8388624 | tf_op jit(solution)/shard_map/all_gather | solution.py:89
  193.9 6.0 multiply_convert_fusion
  199.9 69.2 %all-gather.12.cloned.1.call-done = bf16[4096,1024]{1,0:T(8,128)(2,1)} async-done(((bf16[256,1024]{1,0:T(8,128)(2,1)}), bf16[4096,1024]{1,0:T(8,128)(2,1)}) %all-gather.12.cloned.1.call-update) | async-done | bytes 8388624 | tf_op jit(solution)/shard_map/all_gather | solution.py:90
  269.1 5.2 fusion.84
  328.8 7.4 reduce-scatter.11.cloned.1.call-done
  337.1 13.6 %reduce-scatter.13.cloned.1.call-done = bf16[64,1024]{1,0:T(8,128)(2,1)} async-done(((bf16[128,1024]{1,0:T(8,128)(2,1)}), bf16[64,1024]{1,0:T(8,128)(2,1)}) %reduce-scatter.13.cloned.1.call-update) | async-done | bytes 131088 | tf_op jit(solution)/shard_map/reduce_scatter | solution.py:196
  351.6 13.7 %reduce-scatter.15.cloned.1.call-done = bf16[64,1024]{1,0:T(8,128)(2,1)} async-done(((bf16[128,1024]{1,0:T(8,128)(2,1)}), bf16[64,1024]{1,0:T(8,128)(2,1)}) %reduce-scatter.15.cloned.1.call-update) | async-done | bytes 131088 | tf_op jit(solution)/shard_map/reduce_scatter | solution.py:199
  366.2 6.3 fusion.18
  373.7 8.9 fusion.14
  383.9 8.3 fusion.10
  392.5 49.1 %reduce-scatter.19.cloned.1.call-done = f32[64,1024]{1,0:T(8,128)} async-done(((f32[1024,1024]{1,0:T(8,128)}), f32[64,1024]{1,0:T(8,128)}) %reduce-scatter.19.cloned.1.call-update) | async-done | bytes 262160 | tf_op jit(solution)/shard_map/reduce_scatter | solution.py:233
  443.2 136.5 %reduce-scatter.17.cloned.1.call-done = f32[64,3072]{1,0:T(8,128)} async-done(((f32[1024,3072]{1,0:T(8,128)}), f32[64,3072]{1,0:T(8,128)}) %reduce-scatter.17.cloned.1.call-update) | async-done | bytes 786448 | tf_op jit(solution)/shard_map/reduce_scatter | solution.py:233
  581.6 180.5 %reduce-scatter.23.cloned.1.call-done = f32[256,1024]{1,0:T(8,128)} async-done(((f32[4096,1024]{1,0:T(8,128)}), f32[256,1024]{1,0:T(8,128)}) %reduce-scatter.23.cloned.1.call-update) | async-done | bytes 1048592 | tf_op jit(solution)/shard_map/reduce_scatter | solution.py:233
  764.2 180.0 %reduce-scatter.21.cloned.1.call-done = f32[64,4096]{1,0:T(8,128)} async-done(((f32[1024,4096]{1,0:T(8,128)}), f32[64,4096]{1,0:T(8,128)}) %reduce-scatter.21.cloned.1.call-update) | async-done | bytes 1048592 | tf_op jit(solution)/shard_map/reduce_scatter | solution.py:233
  948.7 59.7 %all-reduce.17 = (bf16[1024]{0:T(1024)(128)(2,1)S(1)}, bf16[1024]{0:T(1024)(128)(2,1)S(1)}, bf16[1024]{0:T(1024)(128)(2,1)S(1)}, bf16[1024]{0:T(1024)(128)(2,1)S...) all-reduce(f32[1024]{0:T(1024)S(1)} %add.318, ...), channel_id=10, replica_groups=mesh['dp'=16,'seq'=2] {'dp'}, use_global_device_ids=true, to_apply=%region_36.0.clone | all-reduce | flops 12288 | bytes 73728
  1009.1 5.2 all-reduce.19
  1019.0 4.8 fusion.5
  1023.8 4.8 fusion.4
  (346 shorter events, 112.1 us)
Async XLA Ops:
  7.2 97.0 %all-gather.6.cloned.1.call-start = ((), (), s32[]{:S(2)}) async-start(), calls=%async_computation.8 | async-start | bytes 6684672 | tf_op jit(solution)/shard_map/all_gather | solution.py:87
  7.9 129.8 %all-gather.8.cloned.1.call-start = ((), (), s32[]{:S(2)}) async-start(), calls=%async_computation.9 | async-start | bytes 2228224 | tf_op jit(solution)/shard_map/all_gather | solution.py:88
  8.7 185.2 %all-gather.10.cloned.1.call-start = ((), (), s32[]{:S(2)}) async-start(), calls=%async_computation.10 | async-start | bytes 8912896 | tf_op jit(solution)/shard_map/all_gather | solution.py:89
  9.4 259.7 %all-gather.12.cloned.1.call-start = ((), (), s32[]{:S(2)}) async-start(), calls=%async_computation.11 | async-start | bytes 8912896 | tf_op jit(solution)/shard_map/all_gather | solution.py:90
  10.0 317.9 %reduce-scatter.9.cloned.1.call-start = ((), (), s32[]{:S(2)}) async-start(), calls=%async_computation.12 | async-start | bytes 393216 | tf_op jit(solution)/shard_map/reduce_scatter | solution.py:196
  312.3 23.9 %reduce-scatter.11.cloned.1.call-start = ((), (), s32[]{:S(2)}) async-start(), calls=%async_computation.13 | async-start | bytes 393216 | tf_op jit(solution)/shard_map/reduce_scatter | solution.py:199
  318.1 32.6 %reduce-scatter.13.cloned.1.call-start = ((), (), s32[]{:S(2)}) async-start(), calls=%async_computation.14 | async-start | bytes 393216 | tf_op jit(solution)/shard_map/reduce_scatter | solution.py:196
  322.0 43.3 %reduce-scatter.15.cloned.1.call-start = ((), (), s32[]{:S(2)}) async-start(), calls=%async_computation.15 | async-start | bytes 393216 | tf_op jit(solution)/shard_map/reduce_scatter | solution.py:199
  323.3 118.3 %reduce-scatter.19.cloned.1.call-start = ((), (), s32[]{:S(2)}) async-start(), calls=%async_computation.17 | async-start | bytes 4456448 | tf_op jit(solution)/shard_map/reduce_scatter | solution.py:233
  326.1 253.5 %reduce-scatter.17.cloned.1.call-start = ((), (), s32[]{:S(2)}) async-start(), calls=%async_computation.16 | async-start | bytes 13369344 | tf_op jit(solution)/shard_map/reduce_scatter | solution.py:233
  372.5 389.5 %reduce-scatter.23.cloned.1.call-start = ((), (), s32[]{:S(2)}) async-start(), calls=%async_computation.19 | async-start | bytes 17825792 | tf_op jit(solution)/shard_map/reduce_scatter | solution.py:233
  382.7 561.5 %reduce-scatter.21.cloned.1.call-start = ((), (), s32[]{:S(2)}) async-start(), calls=%async_computation.18 | async-start | bytes 17825792 | tf_op jit(solution)/shard_map/reduce_scatter | solution.py:233
  392.4 555.4 %copy-start.53 = (f32[4096]{0:T(1024)S(1)}, f32[4096]{0:T(1024)}, u32[]{:S(2)}) copy-start(f32[4096]{0:T(1024)} %get-tuple-element.63) | copy-start | bytes 49156
  392.4 555.4 %copy-start.64 = (f32[1024]{0:T(1024)S(1)}, f32[1024]{0:T(1024)}, u32[]{:S(2)}) copy-start(f32[1024]{0:T(1024)} %get-tuple-element.61) | copy-start | bytes 12292
  392.4 555.4 %copy-start.65 = (f32[1024]{0:T(1024)S(1)}, f32[1024]{0:T(1024)}, u32[]{:S(2)}) copy-start(f32[1024]{0:T(1024)} %get-tuple-element.59) | copy-start | bytes 12292
  392.4 555.4 %copy-start.62 = (f32[1024]{0:T(1024)S(1)}, f32[1024]{0:T(1024)}, u32[]{:S(2)}) copy-start(f32[1024]{0:T(1024)} %get-tuple-element.17) | copy-start | bytes 12292
  392.4 555.4 %copy-start.63 = (f32[1024]{0:T(1024)S(1)}, f32[1024]{0:T(1024)}, u32[]{:S(2)}) copy-start(f32[1024]{0:T(1024)} %get-tuple-element.24) | copy-start | bytes 12292
  392.4 555.5 %copy-start.46 = (bf16[1,64,1024]{2,1,0:T(8,128)(2,1)S(1)}, bf16[1,64,1024]{2,1,0:T(8,128)(2,1)}, u32[]{:S(2)}) copy-start(bf16[1,64,1024]{2,1,0:T(8,128)(2,1)} %get-tuple-element.84) | copy-start | bytes 393220
  392.4 555.5 %copy-start.47 = (bf16[1,64,1024]{2,1,0:T(8,128)(2,1)S(1)}, bf16[1,64,1024]{2,1,0:T(8,128)(2,1)}, u32[]{:S(2)}) copy-start(bf16[1,64,1024]{2,1,0:T(8,128)(2,1)} %get-tuple-element.85) | copy-start | bytes 393220
  392.4 556.2 %copy-start.48 = (bf16[64,1024]{1,0:T(8,128)(2,1)S(1)}, bf16[64,1024]{1,0:T(8,128)(2,1)}, u32[]{:S(2)}) copy-start(bf16[64,1024]{1,0:T(8,128)(2,1)} %reduce-scatter.11.cloned.1.call-done) | copy-start | bytes 393220
  392.4 556.2 %copy-start.49 = (bf16[64,1024]{1,0:T(8,128)(2,1)S(1)}, bf16[64,1024]{1,0:T(8,128)(2,1)}, u32[]{:S(2)}) copy-start(bf16[64,1024]{1,0:T(8,128)(2,1)} %reduce-scatter.15.cloned.1.call-done) | copy-start | bytes 393220
  392.5 626.5 %copy-start.19 = (f32[64,1024]{1,0:T(8,128)S(1)}, f32[64,1024]{1,0:T(8,128)}, u32[]{:S(2)}) copy-start(f32[64,1024]{1,0:T(8,128)} %copy-done.18) | copy-start | bytes 786436
  392.5 626.5 %copy-start.77 = (f32[64]{0:T(128)S(1)}, f32[64]{0:T(128)}, u32[]{:S(2)}) copy-start(f32[64]{0:T(128)} %copy-done.76) | copy-start | bytes 772
  392.5 637.0 %all-reduce.23.cloned.1.call-start = ((), (), s32[]{:S(2)}) async-start(), calls=%async_computation.20 | async-start | bytes 3145728 | tf_op jit(solution)/shard_map/psum | solution.py:235
  (71 other events, 5691.0 us)
Sparse Core Ops, SparseCore 0:
  10.3 65.4 all-gather.5
  78.0 39.9 all-gather.7
  120.2 73.6 all-gather.9
  195.9 73.1 all-gather.11
  312.4 9.8 reduce-scatter.8
  324.5 11.6 reduce-scatter.10
  339.0 11.6 reduce-scatter.12
  353.6 11.6 reduce-scatter.14
  369.1 72.4 reduce-scatter.18
  446.0 133.5 reduce-scatter.16
  584.3 177.6 reduce-scatter.22
  766.6 177.5 reduce-scatter.20
  947.3 51.0 all-reduce.22
where the time goes:
time: 1050 us; the launch traced here: 1040 us
  waiting for transfers between devices  703 us (67%)
  blocking collectives  170 us (16%)
  matrix products  86.8 us (8%)
  other arithmetic  35.1 us (3%)
  local copies, waits for them, and re-layouts  31 us (3%)
  between operations  17.5 us (2%)
    reduce_scatter x4, waiting for transfers between devices, per_device(): shares = lax.psum_scatter(totals, 'dp', scatter_dimension=0, tiled=True)  546 us
    unnamed x2, blocking collectives  124 us
    all_gather x1, waiting for transfers between devices, per_device(): lax.all_gather(shards[3], 'dp', axis=0, tiled=True)  69.2 us
    all_gather x1, waiting for transfers between devices, per_device(): lax.all_gather(shards[2], 'dp', axis=0, tiled=True)  50.2 us
    dot_general x4, matrix products, inner_rows(): lax.dot_general(left, right, (((0,), (0,)), ((), ())), preferred_element_...  26.3 us
    dot_general x8, matrix products, times_back(): lax.dot_general(left, right, (((1,), (1,)), ((), ())), preferred_element_...  25.6 us
    reduce_scatter x2, waiting for transfers between devices, per_device(): lax.psum_scatter(value_part.astype(jnp.bfloat16), 'seq', scatter_dimensio...  21.1 us
  transfers between devices with their start and end apart: 13, of which 9 were waited for; matrix products, arithmetic and copies ran while one was open for 9% of the time, Pallas kernels for 0%

commit v1 on v0

--- a/solution.py
+++ b/solution.py
@@ -1,3 +1,4 @@
+import functools
 import math
 import jax
 import jax.numpy as jnp
@@ -5,6 +6,34 @@
 from jax.sharding import PartitionSpec as P
 
 HEAD = 64
+
+
+def number_the_sizes(state, on_dim):
+    extra, g_now, near = (lax.axis_size("dp"), lax.axis_index("dp"), state.shape[on_dim])
+    samples = [(hop_no, (hop_no + 1) % extra) for hop_no in range(extra)]
+    bank = [(hop_no, (hop_no - 1) % extra) for hop_no in range(extra)]
+    later = jnp.zeros(
+        (*state.shape[:on_dim], extra * near, *state.shape[on_dim + 1 :]), state.dtype
+    )
+    later = lax.dynamic_update_slice_in_dim(later, state, g_now * near, axis=on_dim)
+    local_out = b_now = state
+    u1 = extra // 2
+    kk = 1
+    while kk < u1 + 1:
+        local_out = lax.ppermute(local_out, "dp", samples)
+        later = lax.dynamic_update_slice_in_dim(
+            later, local_out, (g_now - kk) % extra * near, axis=on_dim
+        )
+        if kk < extra - u1:
+            b_now = lax.ppermute(b_now, "dp", bank)
+            later = lax.dynamic_update_slice_in_dim(
+                later, b_now, (g_now + kk) % extra * near, axis=on_dim
+            )
+        kk += 1
+    return later
+
+
+open_the_classes = functools.partial(number_the_sizes, on_dim=0)
 
 
 def for_sending(shard):
@@ -87,7 +116,7 @@
             lax.all_gather(shards[0], "dp", axis=0, tiled=True),
             lax.all_gather(shards[1], "dp", axis=0, tiled=True),
             lax.all_gather(shards[2], "dp", axis=0, tiled=True),
-            lax.all_gather(shards[3], "dp", axis=0, tiled=True),
+            open_the_classes(shards[3]),
             lax.all_gather(shards[4], "dp", axis=0, tiled=True),
             lax.all_gather(shards[5], "dp", axis=0, tiled=True),
             lax.all_gather(shards[6], "dp", axis=0, tiled=True),

time: 1050 us -> 1090 us (1.038)
  starting transfers between devices: 0.74 us -> 42.6 us
  waiting for transfers between devices: 703 us -> 680 us
  local copies, waits for them, and re-layouts: 31 us -> 46.2 us
  matrix products: 86.8 us -> 98 us
    ppermute x0 -> x15, waiting for transfers between devices: none -> 67.9 us  [the longest x8 50.5 us: number_the_sizes(): local_out = lax.ppermute(local_out, 'dp', samples)]
    all_gather x1, waiting for transfers between devices: 50.2 us -> 0.02 us  [per_device(): lax.all_gather(shards[2], 'dp', axis=0, tiled=True)]
    ppermute x0 -> x15, starting transfers between devices: none -> 41.9 us  [the longest x7 21.6 us: number_the_sizes(): b_now = lax.ppermute(b_now, 'dp', bank)]
    all_gather x1, waiting for transfers between devices: 69.2 us -> 29.4 us  [per_device(): lax.all_gather(w_down, 'dp', axis=0, tiled=True)]
    dynamic_update_slice x0 -> x16, local copies, waits for them, and re-layouts: none -> 19.7 us  [the longest x8 10.9 us: number_the_sizes(): lax.dynamic_update_slice_in_dim(later, local_out, (g_now - kk) % extra *...]
  transfers between devices with their start and end apart: 13 -> 28, of which waited for: 9 -> 16; matrix products, arithmetic and copies ran while one was open for 9% -> 12% of each run, Pallas kernels for 0% -> 0%
where the time goes in v1:
time: 1090 us; the launch traced here: 1080 us
  waiting for transfers between devices  680 us (62%)
  blocking collectives  167 us (15%)
  matrix products  98 us (9%)
  local copies, waits for them, and re-layouts  46.2 us (4%)
  starting transfers between devices  42.6 us (4%)
  other arithmetic  30.9 us (3%)
  between operations  17.8 us (2%)
    reduce_scatter x4, waiting for transfers between devices, per_device(): shares = lax.psum_scatter(totals, 'dp', scatter_dimension=0, tiled=True)  546 us
    unnamed x2, blocking collectives  120 us
    ppermute x8, waiting for transfers between devices, number_the_sizes(): local_out = lax.ppermute(local_out, 'dp', samples)  50.5 us
    dot_general x8, matrix products, times_back(): lax.dot_general(left, right, (((1,), (1,)), ((), ())), preferred_element_...  32.7 us
    all_gather x1, waiting for transfers between devices, per_device(): lax.all_gather(w_down, 'dp', axis=0, tiled=True)  29.4 us
    dot_general x4, matrix products, inner_rows(): lax.dot_general(left, right, (((0,), (0,)), ((), ())), preferred_element_...  27.3 us
  transfers between devices with their start and end apart: 28, of which 16 were waited for; matrix products, arithmetic and copies ran while one was open for 12% of the time, Pallas kernels for 0%

profile of v1, /device:TPU:0, one launch (start us, length us, event | category | flops | bytes accessed | tf_op | source)
XLA Modules:
  0.0 1082.2 jit_solution(1283007268162980714)
XLA Ops:
  15.7 7.1 collective-permute-done
  22.8 6.7 collective-permute-start.2
  29.6 15.5 %collective-permute-done.2 = bf16[256,1024]{1,0:T(8,128)(2,1)S(1)} collective-permute-done((bf16[256,1024]{1,0:T(8,128)(2,1)S(1)}, bf16[256,1024]{1,0:T(8,128)(2,1)S(1)}, u32[]{:S(2)}, u32[]{:S(2)}) %collective-permute-start.2) | collective-permute-done | bytes 524320 | tf_op jit(solution)/shard_map/ppermute | solution.py:23
  49.5 11.3 %collective-permute-done.4 = bf16[256,1024]{1,0:T(8,128)(2,1)S(1)} collective-permute-done((bf16[256,1024]{1,0:T(8,128)(2,1)S(1)}, bf16[256,1024]{1,0:T(8,128)(2,1)S(1)}, u32[]{:S(2)}, u32[]{:S(2)}) %collective-permute-start.4) | collective-permute-done | bytes 524320 | tf_op jit(solution)/shard_map/ppermute | solution.py:23
  60.8 6.5 collective-permute-done.5
  83.6 7.4 collective-permute-done.8
  104.5 60.6 %all-reduce.18 = (bf16[1024]{0:T(1024)(128)(2,1)S(1)}, bf16[1024]{0:T(1024)(128)(2,1)S(1)}, bf16[1024]{0:T(1024)(128)(2,1)S(1)}, bf16[1024]{0:T(1024)(128)(2,1)S...) all-reduce(bf16[1024]{0:T(1024)(128)(2,1)S(1)} %dynamic-update-slic, ...), channel_id=1, replica_groups=mesh['dp'=16,'seq'=2] {'dp'}, use_global_device_ids=true, to_apply=%add | all-reduce | flops 8192 | bytes 32768
  165.1 17.2 %all-gather = bf16[16,1,256]{2,1,0:T(2,128)(2,1)S(1)} all-gather(bf16[1,1,256]{2,1,0:T(2,128)(2,1)S(1)} %reshape.260), channel_id=1, replica_groups=mesh['dp'=16,'seq'=2] {'dp'}, dimensions={0}, use_global_device_ids=true | all-gather | bytes 8704 | tf_op jit(solution)/shard_map/all_gather | solution.py:125
  195.4 10.9 %collective-permute-done.11 = bf16[256,1024]{1,0:T(8,128)(2,1)S(1)} collective-permute-done((bf16[256,1024]{1,0:T(8,128)(2,1)S(1)}, bf16[256,1024]{1,0:T(8,128)(2,1)S(1)}, u32[]{:S(2)}, u32[]{:S(2)}) %collective-permute-start.11) | collective-permute-done | bytes 524320 | tf_op jit(solution)/shard_map/ppermute | solution.py:28
  249.1 7.3 all_gather.72
  287.1 29.4 %all-gather.12.cloned.1.call-done = bf16[4096,1024]{1,0:T(8,128)(2,1)} async-done(((bf16[256,1024]{1,0:T(8,128)(2,1)}), bf16[4096,1024]{1,0:T(8,128)(2,1)}) %all-gather.12.cloned.1.call-update) | async-done | bytes 8388624 | tf_op jit(solution)/shard_map/all_gather | solution.py:183
  316.5 7.0 convert_reduce_fusion
  323.5 6.4 convolution_add_fusion.6
  368.0 6.2 reduce-scatter.11.cloned.1.call-done
  375.2 13.6 %reduce-scatter.13.cloned.1.call-done = bf16[64,1024]{1,0:T(8,128)(2,1)} async-done(((bf16[128,1024]{1,0:T(8,128)(2,1)}), bf16[64,1024]{1,0:T(8,128)(2,1)}) %reduce-scatter.13.cloned.1.call-update) | async-done | bytes 131088 | tf_op jit(solution)/shard_map/reduce_scatter | solution.py:225
  389.6 13.7 %reduce-scatter.15.cloned.1.call-done = bf16[64,1024]{1,0:T(8,128)(2,1)} async-done(((bf16[128,1024]{1,0:T(8,128)(2,1)}), bf16[64,1024]{1,0:T(8,128)(2,1)}) %reduce-scatter.15.cloned.1.call-update) | async-done | bytes 131088 | tf_op jit(solution)/shard_map/reduce_scatter | solution.py:228
  404.2 6.3 fusion.18
  411.8 8.9 fusion.14
  421.9 8.4 fusion.10
  430.5 49.1 %reduce-scatter.19.cloned.1.call-done = f32[64,1024]{1,0:T(8,128)} async-done(((f32[1024,1024]{1,0:T(8,128)}), f32[64,1024]{1,0:T(8,128)}) %reduce-scatter.19.cloned.1.call-update) | async-done | bytes 262160 | tf_op jit(solution)/shard_map/reduce_scatter | solution.py:262
  481.3 136.5 %reduce-scatter.17.cloned.1.call-done = f32[64,3072]{1,0:T(8,128)} async-done(((f32[1024,3072]{1,0:T(8,128)}), f32[64,3072]{1,0:T(8,128)}) %reduce-scatter.17.cloned.1.call-update) | async-done | bytes 786448 | tf_op jit(solution)/shard_map/reduce_scatter | solution.py:262
  619.7 180.5 %reduce-scatter.23.cloned.1.call-done = f32[256,1024]{1,0:T(8,128)} async-done(((f32[4096,1024]{1,0:T(8,128)}), f32[256,1024]{1,0:T(8,128)}) %reduce-scatter.23.cloned.1.call-update) | async-done | bytes 1048592 | tf_op jit(solution)/shard_map/reduce_scatter | solution.py:262
  802.3 180.0 %reduce-scatter.21.cloned.1.call-done = f32[64,4096]{1,0:T(8,128)} async-done(((f32[1024,4096]{1,0:T(8,128)}), f32[64,4096]{1,0:T(8,128)}) %reduce-scatter.21.cloned.1.call-update) | async-done | bytes 1048592 | tf_op jit(solution)/shard_map/reduce_scatter | solution.py:262
  986.9 59.7 %all-reduce.17 = (bf16[1024]{0:T(1024)(128)(2,1)S(1)}, bf16[1024]{0:T(1024)(128)(2,1)S(1)}, bf16[1024]{0:T(1024)(128)(2,1)S(1)}, bf16[1024]{0:T(1024)(128)(2,1)S...) all-reduce(f32[1024]{0:T(1024)S(1)} %add.517, ...), channel_id=10, replica_groups=mesh['dp'=16,'seq'=2] {'dp'}, use_global_device_ids=true, to_apply=%region_36.37.clone | all-reduce | flops 12288 | bytes 73728
  (422 shorter events, 208.2 us)
Async XLA Ops:
  7.3 218.0 %all-gather.6.cloned.1.call-start = ((), (), s32[]{:S(2)}) async-start(), calls=%async_computation.8 | async-start | bytes 6684672 | tf_op jit(solution)/shard_map/all_gather | solution.py:116
  8.0 250.9 %all-gather.8.cloned.1.call-start = ((), (), s32[]{:S(2)}) async-start(), calls=%async_computation.9 | async-start | bytes 2228224 | tf_op jit(solution)/shard_map/all_gather | solution.py:117
  8.8 255.7 %all-gather.10.cloned.1.call-start = ((), (), s32[]{:S(2)}) async-start(), calls=%async_computation.10 | async-start | bytes 8912896 | tf_op jit(solution)/shard_map/all_gather | solution.py:118
  9.5 306.9 %all-gather.12.cloned.1.call-start = ((), (), s32[]{:S(2)}) async-start(), calls=%async_computation.11 | async-start | bytes 8912896 | tf_op jit(solution)/shard_map/all_gather | solution.py:183
  10.1 357.0 %reduce-scatter.9.cloned.1.call-start = ((), (), s32[]{:S(2)}) async-start(), calls=%async_computation.12 | async-start | bytes 393216 | tf_op jit(solution)/shard_map/reduce_scatter | solution.py:225
  10.6 18.9 %collective-permute-start.1 = (bf16[256,1024]{1,0:T(8,128)(2,1)}, bf16[256,1024]{1,0:T(8,128)(2,1)S(1)}, u32[]{:S(2)}, u32[]{:S(2)}) collective-permute-start(bf16[256,1024]{1,0:T(8,128)(2,1)} %param.20), channel_id=1, source_target_pairs={{0,30},{2,0},{4,2},{6,4},{8,6},{10,8},{12,10},{14,12},{16,14},{18,... | collective-permute-start | bytes 1572872 | tf_op jit(solution)/shard_map/ppermute | solution.py:28
  22.8 22.2 %collective-permute-start.2 = (bf16[256,1024]{1,0:T(8,128)(2,1)S(1)}, bf16[256,1024]{1,0:T(8,128)(2,1)S(1)}, u32[]{:S(2)}, u32[]{:S(2)}) collective-permute-start(bf16[256,1024]{1,0:T(8,128)(2,1)S(1)} %collective-permute-done), channel_id=1, source_target_pairs={{0,2},{2,4},{4,6},{6,8},{8,10},{10,12},{12,14},{14,16},{16,18},{18... | collective-permute-start | bytes 1572872 | tf_op jit(solution)/shard_map/ppermute | solution.py:23
  29.6 15.5 %collective-permute-start.3 = (bf16[256,1024]{1,0:T(8,128)(2,1)S(1)}, bf16[256,1024]{1,0:T(8,128)(2,1)S(1)}, u32[]{:S(2)}, u32[]{:S(2)}) collective-permute-start(bf16[256,1024]{1,0:T(8,128)(2,1)S(1)} %collective-permute-done.1), channel_id=1, source_target_pairs={{0,30},{2,0},{4,2},{6,4},{8,6},{10,8},{12,10},{14,12},{16,14},{18,... | collective-permute-start | bytes 1572872 | tf_op jit(solution)/shard_map/ppermute | solution.py:28
  45.1 15.7 %collective-permute-start.4 = (bf16[256,1024]{1,0:T(8,128)(2,1)S(1)}, bf16[256,1024]{1,0:T(8,128)(2,1)S(1)}, u32[]{:S(2)}, u32[]{:S(2)}) collective-permute-start(bf16[256,1024]{1,0:T(8,128)(2,1)S(1)} %collective-permute-done.2), channel_id=1, source_target_pairs={{0,2},{2,4},{4,6},{6,8},{8,10},{10,12},{12,14},{14,16},{16,18},{18... | collective-permute-start | bytes 1572872 | tf_op jit(solution)/shard_map/ppermute | solution.py:23
  45.1 22.2 %collective-permute-start.5 = (bf16[256,1024]{1,0:T(8,128)(2,1)S(1)}, bf16[256,1024]{1,0:T(8,128)(2,1)S(1)}, u32[]{:S(2)}, u32[]{:S(2)}) collective-permute-start(bf16[256,1024]{1,0:T(8,128)(2,1)S(1)} %collective-permute-done.3), channel_id=1, source_target_pairs={{0,30},{2,0},{4,2},{6,4},{8,6},{10,8},{12,10},{14,12},{16,14},{18,... | collective-permute-start | bytes 1572872 | tf_op jit(solution)/shard_map/ppermute | solution.py:28
  60.8 16.4 %collective-permute-start.6 = (bf16[256,1024]{1,0:T(8,128)(2,1)S(1)}, bf16[256,1024]{1,0:T(8,128)(2,1)}, u32[]{:S(2)}, u32[]{:S(2)}) collective-permute-start(bf16[256,1024]{1,0:T(8,128)(2,1)S(1)} %collective-permute-done.4), channel_id=1, source_target_pairs={{0,2},{2,4},{4,6},{6,8},{8,10},{10,12},{12,14},{14,16},{16,18},{18... | collective-permute-start | bytes 1572872 | tf_op jit(solution)/shard_map/ppermute | solution.py:23
  67.3 15.7 %collective-permute-start.7 = (bf16[256,1024]{1,0:T(8,128)(2,1)S(1)}, bf16[256,1024]{1,0:T(8,128)(2,1)}, u32[]{:S(2)}, u32[]{:S(2)}) collective-permute-start(bf16[256,1024]{1,0:T(8,128)(2,1)S(1)} %collective-permute-done.5), channel_id=1, source_target_pairs={{0,30},{2,0},{4,2},{6,4},{8,6},{10,8},{12,10},{14,12},{16,14},{18,... | collective-permute-start | bytes 1572872 | tf_op jit(solution)/shard_map/ppermute | solution.py:28
  82.9 104.2 %collective-permute-start.9 = (bf16[256,1024]{1,0:T(8,128)(2,1)}, bf16[256,1024]{1,0:T(8,128)(2,1)S(1)}, u32[]{:S(2)}, u32[]{:S(2)}) collective-permute-start(bf16[256,1024]{1,0:T(8,128)(2,1)} %collective-permute-done.7), channel_id=1, source_target_pairs={{0,30},{2,0},{4,2},{6,4},{8,6},{10,8},{12,10},{14,12},{16,14},{18,... | collective-permute-start | bytes 1572872 | tf_op jit(solution)/shard_map/ppermute | solution.py:28
  91.1 98.9 %collective-permute-start.10 = (bf16[256,1024]{1,0:T(8,128)(2,1)}, bf16[256,1024]{1,0:T(8,128)(2,1)}, u32[]{:S(2)}, u32[]{:S(2)}) collective-permute-start(bf16[256,1024]{1,0:T(8,128)(2,1)} %collective-permute-done.8), channel_id=1, source_target_pairs={{0,2},{2,4},{4,6},{6,8},{8,10},{10,12},{12,14},{14,16},{16,18},{18... | collective-permute-start | bytes 1572872 | tf_op jit(solution)/shard_map/ppermute | solution.py:23
  187.2 19.2 %collective-permute-start.11 = (bf16[256,1024]{1,0:T(8,128)(2,1)S(1)}, bf16[256,1024]{1,0:T(8,128)(2,1)S(1)}, u32[]{:S(2)}, u32[]{:S(2)}) collective-permute-start(bf16[256,1024]{1,0:T(8,128)(2,1)S(1)} %collective-permute-done.9), channel_id=1, source_target_pairs={{0,30},{2,0},{4,2},{6,4},{8,6},{10,8},{12,10},{14,12},{16,14},{18,... | collective-permute-start | bytes 1572872 | tf_op jit(solution)/shard_map/ppermute | solution.py:28
  190.0 22.9 %collective-permute-start.12 = (bf16[256,1024]{1,0:T(8,128)(2,1)}, bf16[256,1024]{1,0:T(8,128)(2,1)S(1)}, u32[]{:S(2)}, u32[]{:S(2)}) collective-permute-start(bf16[256,1024]{1,0:T(8,128)(2,1)} %collective-permute-done.10), channel_id=1, source_target_pairs={{0,2},{2,4},{4,6},{6,8},{8,10},{10,12},{12,14},{14,16},{16,18},{18... | collective-permute-start | bytes 1572872 | tf_op jit(solution)/shard_map/ppermute | solution.py:23
  350.4 23.8 %reduce-scatter.11.cloned.1.call-start = ((), (), s32[]{:S(2)}) async-start(), calls=%async_computation.13 | async-start | bytes 393216 | tf_op jit(solution)/shard_map/reduce_scatter | solution.py:228
  356.3 32.4 %reduce-scatter.13.cloned.1.call-start = ((), (), s32[]{:S(2)}) async-start(), calls=%async_computation.14 | async-start | bytes 393216 | tf_op jit(solution)/shard_map/reduce_scatter | solution.py:225
  360.2 43.1 %reduce-scatter.15.cloned.1.call-start = ((), (), s32[]{:S(2)}) async-start(), calls=%async_computation.15 | async-start | bytes 393216 | tf_op jit(solution)/shard_map/reduce_scatter | solution.py:228
  361.5 118.2 %reduce-scatter.19.cloned.1.call-start = ((), (), s32[]{:S(2)}) async-start(), calls=%async_computation.17 | async-start | bytes 4456448 | tf_op jit(solution)/shard_map/reduce_scatter | solution.py:262
  365.3 252.5 %reduce-scatter.17.cloned.1.call-start = ((), (), s32[]{:S(2)}) async-start(), calls=%async_computation.16 | async-start | bytes 13369344 | tf_op jit(solution)/shard_map/reduce_scatter | solution.py:262
  410.6 389.7 %reduce-scatter.23.cloned.1.call-start = ((), (), s32[]{:S(2)}) async-start(), calls=%async_computation.19 | async-start | bytes 17825792 | tf_op jit(solution)/shard_map/reduce_scatter | solution.py:262
  420.7 561.6 %reduce-scatter.21.cloned.1.call-start = ((), (), s32[]{:S(2)}) async-start(), calls=%async_computation.18 | async-start | bytes 17825792 | tf_op jit(solution)/shard_map/reduce_scatter | solution.py:262
  430.5 637.2 %all-reduce.23.cloned.1.call-start = ((), (), s32[]{:S(2)}) async-start(), calls=%async_computation.20 | async-start | bytes 3145728 | tf_op jit(solution)/shard_map/psum | solution.py:264
  (99 other events, 12226.3 us)
Sparse Core Ops, SparseCore 0:
  10.4 91.9 all-gather.5
  104.6 41.6 all-gather.7
  148.4 93.0 all-gather.9
  243.5 72.8 all-gather.11
  350.6 9.7 reduce-scatter.8
  362.5 11.6 reduce-scatter.10
  377.0 11.6 reduce-scatter.12
  391.6 11.6 reduce-scatter.14
  407.2 72.4 reduce-scatter.18
  484.1 133.6 reduce-scatter.16
  622.5 177.7 reduce-scatter.22
  804.8 177.5 reduce-scatter.20
  985.5 51.0 all-reduce.22
